TPU v7x, 512 devices: a whole 4x8x8 slice. The times are simulated.
512 devices in a mesh: dp: 8 (over z), expert: 64 (over x, y, core).
Axes of the slice: x: 4, y: 8, z: 8, core: 2. Of those that a mesh axis runs over, the one named last changes fastest.
Arguments:
- tokens: bfloat16 [65536, 1024], P(('dp', 'expert')), may hold values from -6 to 6
- d_output: bfloat16 [65536, 1024], P(('dp', 'expert')), may hold values from -6 to 6
- combine: float32 [65536, 8], P(('dp', 'expert')), may hold values from 0.05 to 1
- routes: int32 [65536, 8], P(('dp', 'expert')), may hold values from 0 to 63, all different within a row; in each aligned block of 128 rows (0 to 127, 128 to 255, ...) at most 18 rows name the same one
- gate_weight: bfloat16 [64, 1024, 384], P('expert', 'dp'), may hold values from -0.1875 to 0.1875
- up_weight: bfloat16 [64, 1024, 384], P('expert', 'dp'), may hold values from -0.1875 to 0.1875
- down_weight: bfloat16 [64, 384, 1024], P('expert', None, 'dp'), may hold values from -0.3125 to 0.3125
Outputs:
- d_tokens: bfloat16 [65536, 1024], P(('dp', 'expert'))
- d_gate_weight: float32 [64, 1024, 384], P('expert', 'dp')
- d_up_weight: float32 [64, 1024, 384], P('expert', 'dp')
- d_down_weight: float32 [64, 384, 1024], P('expert', None, 'dp')
Inputs may be any that keep to these rules, and one draw needn't show every extreme that they name: `routes`: among the 128 tokens of one device, each expert id is named by at most 18 rows; some expert is named by exactly 18 rows on some device. The ids of one token differ.
All inputs are finite; a program needn't handle non-finite values.
Results may differ from a plain program's by a relative error of at most 0.015.
Values may be sent and summed in bfloat16 or wider, within the bound.
A program may use at most 64 MiB of HBM per device.

v0:
```python
import jax
import jax.numpy as jnp
from jax import lax
from jax.sharding import PartitionSpec as P


def route_slots(routes, experts):
    matches = (routes[:, :, None] == jnp.arange(experts, dtype=jnp.int32)[None, None, :]).astype(
        jnp.int32
    )
    per_token = jnp.sum(matches, axis=1)
    earlier = jnp.cumsum(per_token, axis=0) - per_token
    return jnp.sum(matches * earlier[:, None, :], axis=2)


def row_work(row_inputs, row_grads, gate_up, down_matrix):
    hidden_units = down_matrix.shape[0]
    preact = jnp.dot(row_inputs, gate_up, preferred_element_type=jnp.float32)
    gate_pre = preact[:, :hidden_units]
    up_pre = preact[:, hidden_units:]
    gate_sigmoid = jax.nn.sigmoid(gate_pre)
    hidden = (gate_pre * gate_sigmoid * up_pre).astype(jnp.bfloat16)
    d_hidden = jnp.dot(row_grads, down_matrix.T, preferred_element_type=jnp.float32)
    d_gate_pre = d_hidden * up_pre * gate_sigmoid * (1.0 + gate_pre * (1.0 - gate_sigmoid))
    d_up_pre = d_hidden * gate_pre * gate_sigmoid
    d_preact = jnp.concatenate([d_gate_pre, d_up_pre], axis=1).astype(jnp.bfloat16)
    d_rows = jnp.dot(d_preact, gate_up.T, preferred_element_type=jnp.float32).astype(jnp.bfloat16)
    return (d_rows, hidden, d_preact)


def body(tokens, d_output, combine, routes, gate_weight, up_weight, down_weight):
    experts = lax.axis_size("expert")
    tok_count = tokens.shape[0]
    model_width = tokens.shape[1]
    top_count = routes.shape[1]
    capacity = max(2, (9 * tok_count * top_count + 8 * experts - 1) // (8 * experts))
    slot_count = experts * capacity
    slot_index = route_slots(routes, experts)
    position = (routes * capacity + slot_index).reshape(-1)
    spread_inputs = jnp.repeat(tokens, top_count, axis=0)
    scaled = (
        (combine[:, :, None] * d_output[:, None, :].astype(jnp.float32))
        .astype(jnp.bfloat16)
        .reshape(-1, model_width)
    )
    send_inputs = (
        jnp.zeros((slot_count, model_width), jnp.bfloat16)
        .at[position]
        .set(spread_inputs)
        .reshape(experts, capacity, model_width)
    )
    send_grads = (
        jnp.zeros((slot_count, model_width), jnp.bfloat16)
        .at[position]
        .set(scaled)
        .reshape(experts, capacity, model_width)
    )
    whole_gate, whole_up, whole_down = (
        lax.all_gather(gate_weight, "dp", axis=1, tiled=True),
        lax.all_gather(up_weight, "dp", axis=1, tiled=True),
        lax.all_gather(down_weight, "dp", axis=2, tiled=True),
    )
    gate_up = jnp.concatenate([whole_gate[0], whole_up[0]], axis=1)
    down_matrix = whole_down[0]
    hidden_units = down_matrix.shape[0]
    recv_inputs, recv_grads = (
        lax.all_to_all(send_inputs, "expert", split_axis=0, concat_axis=0, tiled=True),
        lax.all_to_all(send_grads, "expert", split_axis=0, concat_axis=0, tiled=True),
    )
    flat_inputs = recv_inputs.reshape(-1, model_width)
    flat_grads = recv_grads.reshape(-1, model_width)
    d_rows, hidden, d_preact = row_work(flat_inputs, flat_grads, gate_up, down_matrix)
    returned = lax.all_to_all(
        d_rows.reshape(experts, capacity, model_width),
        "expert",
        split_axis=0,
        concat_axis=0,
        tiled=True,
    )
    route_rows = returned.reshape(-1, model_width)[position].reshape(
        tok_count, top_count, model_width
    )
    d_tokens = jnp.sum(route_rows.astype(jnp.float32), axis=1).astype(jnp.bfloat16)
    gate_up_grad = jnp.dot(flat_inputs.T, d_preact, preferred_element_type=jnp.float32)
    down_grad = jnp.dot(flat_grads.T, hidden, preferred_element_type=jnp.float32)
    stacked = jnp.concatenate([gate_up_grad, down_grad], axis=1)
    summed = lax.psum_scatter(
        stacked.astype(jnp.bfloat16), "dp", scatter_dimension=0, tiled=True
    ).astype(jnp.float32)
    d_gate_weight = summed[:, :hidden_units][None]
    d_up_weight = summed[:, hidden_units : 2 * hidden_units][None]
    d_down_weight = summed[:, 2 * hidden_units :].T[None]
    return (d_tokens, d_gate_weight, d_up_weight, d_down_weight)


def solution(mesh):
    placed = (
        P(("dp", "expert"), None),
        P(("dp", "expert"), None),
        P(("dp", "expert"), None),
        P(("dp", "expert"), None),
        P("expert", "dp", None),
        P("expert", "dp", None),
        P("expert", None, "dp"),
    )
    return jax.shard_map(
        body,
        mesh=mesh,
        in_specs=placed,
        out_specs=(
            P(("dp", "expert"), None),
            P("expert", "dp", None),
            P("expert", "dp", None),
            P("expert", None, "dp"),
        ),
        check_vma=False,
    )
```

profile of v0, /device:TPU:1, one launch (start us, length us, event | category | flops | bytes accessed | tf_op | source)
XLA Modules:
  0.0 330.5 jit_solution(18078661174576874476)
XLA Ops:
  7.2 0.0 copy-start
  7.2 0.8 convert_reduce_fusion
  7.9 0.1 copy.24
  8.0 0.2 reduce_window_sum.11
  8.2 0.1 copy.26
  8.3 0.7 select_reduce_fusion
  9.0 0.7 multiply_add_fusion
  9.7 0.1 copy.27
  9.8 0.1 reshape.80
  10.0 0.0 copy-done
  10.0 6.0 %scatter_custom_fusion.1 = bf16[1152,1024]{1,0:T(8,128)(2,1)S(1)} fusion(s32[1024]{0:T(1024)S(1)} %bitcast.37, bf16[]{:T(256)} %constant.5.clone.1, bf16[128,1024]{1,0:T(8,128)(2,1)S(1)} %copy-done), kind=kCustom, calls=%fused_computation.9 | custom fusion | bytes 2621442 | tf_op jit(solution)/shard_map/scatter | solution.py:49
  16.0 2.4 reshape.84
  18.4 0.0 copy-start.6
  18.4 11.8 %all-to-all-start.1 = ((bf16[64,18,1024]{2,1,0:T(8,128)(2,1)}), bf16[64,18,1024]{2,1,0:T(8,128)(2,1)S(1)}, u32[]{:S(2)}, u32[]{:S(2)}) async-start(bf16[64,18,1024]{2,1,0:T(8,128)(2,1)} %reshape.84), calls=%async_computation.1 | async-start | bytes 6291456 | tf_op jit(solution)/shard_map/all_to_all | solution.py:67
  30.2 0.0 copy-done.6
  30.2 0.1 copy.28
  30.3 0.1 mul.60
  30.4 1.8 convert_element_type.25
  32.2 7.7 %scatter_custom_fusion = bf16[1152,1024]{1,0:T(8,128)(2,1)} fusion(s32[1024]{0:T(1024)S(1)} %bitcast.38, f32[128,1024]{1,0:T(8,128)} %convert_element_type.25, f32[1024]{0:T(1024)S(1)} %mul.60, bf16[]{:T(256)} %constant.5.clone.1), kind=kCustom, calls=%fused_computation.7 | custom fusion | flops 2097152 | bytes 2887682 | tf_op jit(solution)/shard_map/scatter | solution.py:55
  39.9 4.3 %reshape.81 = bf16[64,18,1024]{2,1,0:T(8,128)(2,1)} reshape(bf16[1152,1024]{1,0:T(8,128)(2,1)} %scatter_custom_fusion) | data formatting | bytes 4718592 | tf_op jit(solution)/shard_map/reshape | solution.py:56
  44.2 0.0 copy-start.5
  44.2 59.5 %all-to-all-done.1 = bf16[64,18,1024]{2,1,0:T(8,128)(2,1)S(1)} async-done(((bf16[64,18,1024]{2,1,0:T(8,128)(2,1)}), bf16[64,18,1024]{2,1,0:T(8,128)(2,1)S(1)}, u32[]{:S(2)}, u32[]{:S(2)}) %all-to-all-start.1) | async-done | bytes 2359328 | tf_op jit(solution)/shard_map/all_to_all | solution.py:67
  103.7 6.2 %all-to-all-start = ((bf16[64,18,1024]{2,1,0:T(8,128)(2,1)}), bf16[64,18,1024]{2,1,0:T(8,128)(2,1)}, u32[]{:S(2)}, u32[]{:S(2)}) async-start(bf16[64,18,1024]{2,1,0:T(8,128)(2,1)} %reshape.81), calls=%async_computation | async-start | bytes 6291456 | tf_op jit(solution)/shard_map/all_to_all | solution.py:68
  109.9 0.0 copy-done.5
  109.9 30.3 %all_gather.10 = bf16[1,1024,384]{2,1,0:T(8,128)(2,1)} all-gather(bf16[1,128,384]{2,1,0:T(8,128)(2,1)S(1)} %copy-done.5), channel_id=1, replica_groups=mesh['dp'=8,'expert'=64] {'dp'}, dimensions={1}, use_global_device_ids=true | all-gather | bytes 884736 | tf_op jit(solution)/shard_map/all_gather | solution.py:59
  140.2 24.1 %all_gather.11 = bf16[1,1024,384]{2,1,0:T(8,128)(2,1)} all-gather(bf16[1,128,384]{2,1,0:T(8,128)(2,1)} %param.12), channel_id=1, replica_groups=mesh['dp'=8,'expert'=64] {'dp'}, dimensions={1}, use_global_device_ids=true | all-gather | bytes 884736 | tf_op jit(solution)/shard_map/all_gather | solution.py:60
  164.3 22.5 %all_gather.9 = bf16[1,384,1024]{2,1,0:T(8,128)(2,1)} all-gather(bf16[1,384,128]{2,1,0:T(8,128)(2,1)} %param.13), channel_id=1, replica_groups=mesh['dp'=8,'expert'=64] {'dp'}, dimensions={2}, use_global_device_ids=true | all-gather | bytes 884736 | tf_op jit(solution)/shard_map/all_gather | solution.py:61
  186.8 2.2 reshape.85
  189.0 6.1 %fusion.10 = f32[1152,768]{0,1:T(8,128)} fusion(bf16[1152,1024]{1,0:T(8,128)(2,1)} %reshape.85, bf16[1024,384]{1,0:T(8,128)(2,1)} %bitcast.35, bf16[1024,384]{1,0:T(8,128)(2,1)} %bitcast.33), kind=kOutput, calls=%fused_computation.24 | convolution fusion | flops 1815085056 | bytes 7471104 | tf_op jit(solution)/shard_map/dot_general | solution.py:18
  195.1 0.0 all-to-all-done
  195.1 2.9 reshape.82
  198.1 0.0 copy-start.4
  198.1 0.0 copy-start.7
  198.1 3.4 %convolution_convert_fusion.2 = bf16[1024,384]{0,1:T(8,128)(2,1)S(1)} fusion(bf16[1152,1024]{1,0:T(8,128)(2,1)S(1)} %reshape.82, f32[1152,768]{0,1:T(8,128)} %fusion.10), kind=kOutput, calls=%fused_computation.20 | convolution fusion | flops 909017088 | bytes 6684672 | tf_op jit(solution)/shard_map/dot_general | solution.py:85
  201.5 0.0 copy-done.4
  201.5 0.0 copy-done.7
  201.5 0.0 copy-start.1
  201.5 1.6 multiply_convert_fusion.2
  203.1 0.0 copy-done.1
  203.1 0.0 copy-start.2
  203.1 0.0 copy-start.3
  203.2 3.3 %convolution_convert_fusion.1 = bf16[1024,768]{0,1:T(8,128)(2,1)} fusion(bf16[1152,1024]{1,0:T(8,128)(2,1)S(1)} %copy-done.1, bf16[1152,384]{0,1:T(8,128)(2,1)S(1)} %get-tuple-element.21, bf16[1152,384]{0,1:T(8,128)(2,1)S(1)} %get-tuple-element.20), kind=kOutput, calls=%fused_computation.18 | convolution fusion | flops 1816264704 | bytes 5701632 | tf_op jit(solution)/shard_map/dot_general | solution.py:84
  206.5 0.0 copy-done.2
  206.5 0.0 copy-done.3
  206.5 2.1 convolution_convert_fusion
  208.6 2.5 reshape.86
  211.0 23.6 %all-to-all-start.2 = ((bf16[64,18,1024]{2,1,0:T(8,128)(2,1)}), bf16[64,18,1024]{2,1,0:T(8,128)(2,1)}, u32[]{:S(2)}, u32[]{:S(2)}) async-start(bf16[64,18,1024]{2,1,0:T(8,128)(2,1)} %reshape.86), calls=%async_computation.2 | async-start | bytes 6291456 | tf_op jit(solution)/shard_map/all_to_all | solution.py:73
  234.7 0.3 reduce-scatter.4.cloned.1.call-start
  234.9 1.6 pad_maximum_fusion
  236.5 2.5 copy.31
  239.1 0.0 reduce-scatter.4.cloned.1.call-update
  239.1 69.0 %all-to-all-done.2 = bf16[64,18,1024]{2,1,0:T(8,128)(2,1)} async-done(((bf16[64,18,1024]{2,1,0:T(8,128)(2,1)}), bf16[64,18,1024]{2,1,0:T(8,128)(2,1)}, u32[]{:S(2)}, u32[]{:S(2)}) %all-to-all-start.2) | async-done | bytes 2359328 | tf_op jit(solution)/shard_map/all_to_all | solution.py:73
  308.1 2.9 reshape.87
  311.0 5.4 %gather_fusion = bf16[1024,1024]{1,0:T(8,128)(2,1)} fusion(bf16[1152,1024]{1,0:T(8,128)(2,1)S(1)} %reshape.87, s32[1024]{0:T(1024)S(1)} %broadcast_clamp_fusion), kind=kCustom, calls=%fused_computation | custom fusion | bytes 4198400 | tf_op jit(solution)/shard_map/gather | solution.py:80
  316.4 3.7 %bitcast_reduce_fusion = bf16[128,1024]{1,0:T(8,128)(2,1)} fusion(bf16[1024,1024]{1,0:T(8,128)(2,1)} %gather_fusion), kind=kLoop, calls=%fused_computation.8 | loop fusion | flops 917504 | bytes 2359296 | tf_op jit(solution)/shard_map/reduce_sum | solution.py:83
  320.1 0.0 reduce-scatter.4.cloned.1.call-done
  320.1 1.2 copy.32
  321.3 0.7 slice_bitcast_fusion
  322.1 0.8 copy.30
  322.9 0.8 copy.29
  (4 shorter events, 0.1 us)
Async XLA Ops:
  7.2 2.8 copy-start
  18.4 11.8 %copy-start.6 = (f32[128,8]{0,1:T(8,128)S(1)}, f32[128,8]{0,1:T(8,128)}, u32[]{:S(2)}) copy-start(f32[128,8]{0,1:T(8,128)} %param.9) | copy-start | bytes 12292
  18.4 85.3 %all-to-all-start.1 = ((bf16[64,18,1024]{2,1,0:T(8,128)(2,1)}), bf16[64,18,1024]{2,1,0:T(8,128)(2,1)S(1)}, u32[]{:S(2)}, u32[]{:S(2)}) async-start(bf16[64,18,1024]{2,1,0:T(8,128)(2,1)} %reshape.84), calls=%async_computation.1 | async-start | bytes 6291456 | tf_op jit(solution)/shard_map/all_to_all | solution.py:67
  44.2 65.8 %copy-start.5 = (bf16[1,128,384]{2,1,0:T(8,128)(2,1)S(1)}, bf16[1,128,384]{2,1,0:T(8,128)(2,1)}, u32[]{:S(2)}) copy-start(bf16[1,128,384]{2,1,0:T(8,128)(2,1)} %param.11) | copy-start | bytes 294916
  103.7 91.5 %all-to-all-start = ((bf16[64,18,1024]{2,1,0:T(8,128)(2,1)}), bf16[64,18,1024]{2,1,0:T(8,128)(2,1)}, u32[]{:S(2)}, u32[]{:S(2)}) async-start(bf16[64,18,1024]{2,1,0:T(8,128)(2,1)} %reshape.81), calls=%async_computation | async-start | bytes 6291456 | tf_op jit(solution)/shard_map/all_to_all | solution.py:68
  198.1 3.4 %copy-start.4 = (bf16[1,384,1024]{2,1,0:T(8,128)(2,1)S(1)}, bf16[1,384,1024]{2,1,0:T(8,128)(2,1)}, u32[]{:S(2)}) copy-start(bf16[1,384,1024]{2,1,0:T(8,128)(2,1)} %all_gather.9) | copy-start | bytes 2359300
  198.1 3.4 %copy-start.7 = (f32[1152,768]{0,1:T(8,128)S(1)}, f32[1152,768]{0,1:T(8,128)}, u32[]{:S(2)}) copy-start(f32[1152,768]{0,1:T(8,128)} %fusion.10) | copy-start | bytes 10616836
  201.5 1.7 copy-start.1
  203.1 3.3 %copy-start.2 = (bf16[1,1024,384]{2,1,0:T(8,128)(2,1)S(1)}, bf16[1,1024,384]{2,1,0:T(8,128)(2,1)}, u32[]{:S(2)}) copy-start(bf16[1,1024,384]{2,1,0:T(8,128)(2,1)} %all_gather.10) | copy-start | bytes 2359300
  203.1 3.3 %copy-start.3 = (bf16[1,1024,384]{2,1,0:T(8,128)(2,1)S(1)}, bf16[1,1024,384]{2,1,0:T(8,128)(2,1)}, u32[]{:S(2)}) copy-start(bf16[1,1024,384]{2,1,0:T(8,128)(2,1)} %all_gather.11) | copy-start | bytes 2359300
  211.0 97.1 %all-to-all-start.2 = ((bf16[64,18,1024]{2,1,0:T(8,128)(2,1)}), bf16[64,18,1024]{2,1,0:T(8,128)(2,1)}, u32[]{:S(2)}, u32[]{:S(2)}) async-start(bf16[64,18,1024]{2,1,0:T(8,128)(2,1)} %reshape.86), calls=%async_computation.2 | async-start | bytes 6291456 | tf_op jit(solution)/shard_map/all_to_all | solution.py:73
  234.7 85.5 %reduce-scatter.4.cloned.1.call-start = ((), (), s32[]{:S(2)}) async-start(), calls=%async_computation.4 | async-start | bytes 2654208
Sparse Core Ops, SparseCore 0:
  239.2 41.3 reduce-scatter.3
where the time goes:
time: 331 us
  waiting for transfers between devices  129 us (39%)
  blocking collectives  76.9 us (23%)
  starting transfers between devices  41.9 us (13%)
  local copies, waits for them, and re-layouts  35.3 us (11%)
  other arithmetic  17.3 us (5%)
  matrix products  16.5 us (5%)
  between operations  14.2 us (4%)
    all_to_all x1, waiting for transfers between devices, body(): lax.all_to_all(d_rows.reshape(experts, capacity, model_width), 'expert',...  69 us
    all_to_all x1, waiting for transfers between devices, body(): lax.all_to_all(send_inputs, 'expert', split_axis=0, concat_axis=0, tiled=...  59.5 us
    all_gather x1, blocking collectives, body(): lax.all_gather(gate_weight, 'dp', axis=1, tiled=True)  30.3 us
    all_gather x1, blocking collectives, body(): lax.all_gather(up_weight, 'dp', axis=1, tiled=True)  24.1 us
    all_to_all x1, starting transfers between devices, body(): lax.all_to_all(d_rows.reshape(experts, capacity, model_width), 'expert',...  23.6 us
    all_gather x1, blocking collectives, body(): lax.all_gather(down_weight, 'dp', axis=2, tiled=True)  22.5 us
    all_to_all x1, starting transfers between devices, body(): lax.all_to_all(send_inputs, 'expert', split_axis=0, concat_axis=0, tiled=...  11.8 us
    scatter x1, other arithmetic, body(): send_grads = jnp.zeros((slot_count, model_width), jnp.bfloat16).at[positi...  7.71 us
  transfers between devices with their start and end apart: 4, of which 2 were waited for; matrix products, arithmetic and copies ran while one was open for 12% of the time, Pallas kernels for 0%

commit v1 on v0

--- a/solution.py
+++ b/solution.py
@@ -2,6 +2,22 @@
 import jax.numpy as jnp
 from jax import lax
 from jax.sharding import PartitionSpec as P
+
+
+def gather_around(x, axis, dim):
+    ways, here, turn = (lax.axis_size(axis), lax.axis_index(axis), x.shape[dim])
+    lengths = [n * ways if d == dim else n for d, n in enumerate(x.shape)]
+    full = lax.dynamic_update_slice_in_dim(jnp.zeros(lengths, x.dtype), x, here * turn, axis=dim)
+    going_up = going_down = x
+    for far in range(1, ways // 2 + 1):
+        going_up = lax.ppermute(going_up, axis, [(d, (d + 1) % ways) for d in range(ways)])
+        full = lax.dynamic_update_slice_in_dim(full, going_up, (here - far) % ways * turn, axis=dim)
+        if 2 * far < ways:
+            going_down = lax.ppermute(going_down, axis, [(d, (d - 1) % ways) for d in range(ways)])
+            full = lax.dynamic_update_slice_in_dim(
+                full, going_down, (here + far) % ways * turn, axis=dim
+            )
+    return full
 
 
 def route_slots(routes, experts):
@@ -56,7 +72,7 @@
         .reshape(experts, capacity, model_width)
     )
     whole_gate, whole_up, whole_down = (
-        lax.all_gather(gate_weight, "dp", axis=1, tiled=True),
+        gather_around(gate_weight, "dp", 1),
         lax.all_gather(up_weight, "dp", axis=1, tiled=True),
         lax.all_gather(down_weight, "dp", axis=2, tiled=True),
     )

time: 331 us -> 347 us (1.048)
  blocking collectives: 76.9 us -> 47.6 us
  starting transfers between devices: 41.9 us -> 67.5 us
  local copies, waits for them, and re-layouts: 35.3 us -> 44.6 us
  waiting for transfers between devices: 129 us -> 135 us
    all_gather x1 -> x0, blocking collectives: 30.3 us -> none  [body(): lax.all_gather(gate_weight, 'dp', axis=1, tiled=True)]
    ppermute x0 -> x7, starting transfers between devices: none -> 26.9 us  [the longest x3 19 us: gather_around(): lax.ppermute(going_down, axis, [(d, (d - 1) % ways) for d in range(ways)])]
    dynamic_update_slice x0 -> x8, local copies, waits for them, and re-layouts: none -> 6.99 us  [the longest x4 3.51 us: gather_around(): lax.dynamic_update_slice_in_dim(full, going_up, (here - far) % ways * tur...]
    ppermute x0 -> x7, waiting for transfers between devices: none -> 6.49 us  [the longest x4 6.48 us: gather_around(): lax.ppermute(going_up, axis, [(d, (d + 1) % ways) for d in range(ways)])]
  transfers between devices with their start and end apart: 4 -> 11, of which waited for: 2 -> 4; matrix products, arithmetic and copies ran while one was open for 12% -> 13% of each run, Pallas kernels for 0% -> 0%
where the time goes in v1:
time: 347 us; the launch traced here: 346 us
  waiting for transfers between devices  135 us (39%)
  starting transfers between devices  67.5 us (19%)
  blocking collectives  47.6 us (14%)
  local copies, waits for them, and re-layouts  44.6 us (13%)
  matrix products  19.4 us (6%)
  other arithmetic  17.3 us (5%)
  between operations  14.3 us (4%)
    all_to_all x1, waiting for transfers between devices, body(): lax.all_to_all(d_rows.reshape(experts, capacity, model_width), 'expert',...  68.9 us
    all_to_all x1, waiting for transfers between devices, body(): lax.all_to_all(send_inputs, 'expert', split_axis=0, concat_axis=0, tiled=...  59.5 us
    all_gather x1, blocking collectives, body(): lax.all_gather(up_weight, 'dp', axis=1, tiled=True)  24.6 us
    all_gather x1, blocking collectives, body(): lax.all_gather(down_weight, 'dp', axis=2, tiled=True)  23 us
    all_to_all x1, starting transfers between devices, body(): lax.all_to_all(d_rows.reshape(experts, capacity, model_width), 'expert',...  22.3 us
    ppermute x3, starting transfers between devices, gather_around(): lax.ppermute(going_down, axis, [(d, (d - 1) % ways) for d in range(ways)])  19 us
    all_to_all x1, starting transfers between devices, body(): lax.all_to_all(send_inputs, 'expert', split_axis=0, concat_axis=0, tiled=...  11.8 us
    ppermute x4, starting transfers between devices, gather_around(): lax.ppermute(going_up, axis, [(d, (d + 1) % ways) for d in range(ways)])  7.85 us
  transfers between devices with their start and end apart: 11, of which 4 were waited for; matrix products, arithmetic and copies ran while one was open for 13% of the time, Pallas kernels for 0%

profile of v1, /device:TPU:1, one launch (start us, length us, event | category | flops | bytes accessed | tf_op | source)
XLA Modules:
  0.0 345.6 jit_solution(15229145057112974437)
XLA Ops:
  7.2 0.0 copy-start
  7.2 0.8 convert_reduce_fusion
  7.9 0.1 copy.24
  8.0 0.2 reduce_window_sum.11
  8.2 0.1 copy.26
  8.3 0.7 select_reduce_fusion
  9.0 0.7 multiply_add_fusion
  9.7 0.1 copy.27
  9.8 0.1 reshape.96
  10.0 6.0 %scatter_custom_fusion.1 = bf16[1152,1024]{1,0:T(8,128)(2,1)S(1)} fusion(s32[1024]{0:T(1024)S(1)} %bitcast.50, bf16[]{:T(256)} %constant.69.clone.1, bf16[128,1024]{1,0:T(8,128)(2,1)S(1)} %copy-done), kind=kCustom, calls=%fused_computation.9 | custom fusion | bytes 2621442 | tf_op jit(solution)/shard_map/scatter | solution.py:65
  16.0 2.4 reshape.100
  18.4 11.8 %all-to-all-start.1 = ((bf16[64,18,1024]{2,1,0:T(8,128)(2,1)}), bf16[64,18,1024]{2,1,0:T(8,128)(2,1)S(1)}, u32[]{:S(2)}, u32[]{:S(2)}) async-start(bf16[64,18,1024]{2,1,0:T(8,128)(2,1)} %reshape.100), calls=%async_computation.1 | async-start | bytes 6291456 | tf_op jit(solution)/shard_map/all_to_all | solution.py:83
  30.2 0.1 copy.28
  30.3 0.1 mul.84
  30.4 1.8 convert_element_type.25
  32.2 7.7 %scatter_custom_fusion = bf16[1152,1024]{1,0:T(8,128)(2,1)} fusion(s32[1024]{0:T(1024)S(1)} %bitcast.51, f32[128,1024]{1,0:T(8,128)} %convert_element_type.25, f32[1024]{0:T(1024)S(1)} %mul.84, bf16[]{:T(256)} %constant.69.clone.1), kind=kCustom, calls=%fused_computation.7 | custom fusion | flops 2097152 | bytes 2887682 | tf_op jit(solution)/shard_map/scatter | solution.py:71
  39.9 4.3 %reshape.97 = bf16[64,18,1024]{2,1,0:T(8,128)(2,1)} reshape(bf16[1152,1024]{1,0:T(8,128)(2,1)} %scatter_custom_fusion) | data formatting | bytes 4718592 | tf_op jit(solution)/shard_map/reshape | solution.py:72
  44.2 59.5 %all-to-all-done.1 = bf16[64,18,1024]{2,1,0:T(8,128)(2,1)S(1)} async-done(((bf16[64,18,1024]{2,1,0:T(8,128)(2,1)}), bf16[64,18,1024]{2,1,0:T(8,128)(2,1)S(1)}, u32[]{:S(2)}, u32[]{:S(2)}) %all-to-all-start.1) | async-done | bytes 2359328 | tf_op jit(solution)/shard_map/all_to_all | solution.py:83
  103.6 6.2 %all-to-all-start = ((bf16[64,18,1024]{2,1,0:T(8,128)(2,1)}), bf16[64,18,1024]{2,1,0:T(8,128)(2,1)}, u32[]{:S(2)}, u32[]{:S(2)}) async-start(bf16[64,18,1024]{2,1,0:T(8,128)(2,1)} %reshape.97), calls=%async_computation | async-start | bytes 6291456 | tf_op jit(solution)/shard_map/all_to_all | solution.py:84
  109.9 10.7 %collective-permute-start.1 = (bf16[1,128,384]{2,1,0:T(8,128)(2,1)}, bf16[1,128,384]{2,1,0:T(8,128)(2,1)}, u32[]{:S(2)}, u32[]{:S(2)}) collective-permute-start(bf16[1,128,384]{2,1,0:T(8,128)(2,1)} %param.11), channel_id=1, source_target_pairs={{0,448},{64,0},{128,64},{192,128},{256,192},{320,256},{384,320},{4... | collective-permute-start | bytes 294920 | tf_op jit(solution)/shard_map/ppermute | solution.py:16
  120.6 1.9 collective-permute-start
  122.5 0.0 copy-start.6
  122.5 24.6 %all_gather.7 = bf16[1,1024,384]{2,1,0:T(8,128)(2,1)} all-gather(bf16[1,128,384]{2,1,0:T(8,128)(2,1)S(1)} %copy-done.5), channel_id=1, replica_groups=mesh['dp'=8,'expert'=64] {'dp'}, dimensions={1}, use_global_device_ids=true | all-gather | bytes 884736 | tf_op jit(solution)/shard_map/all_gather | solution.py:76
  147.1 23.0 %all_gather.6 = bf16[1,384,1024]{2,1,0:T(8,128)(2,1)} all-gather(bf16[1,384,128]{2,1,0:T(8,128)(2,1)} %param.13), channel_id=1, replica_groups=mesh['dp'=8,'expert'=64] {'dp'}, dimensions={2}, use_global_device_ids=true | all-gather | bytes 884736 | tf_op jit(solution)/shard_map/all_gather | solution.py:77
  170.1 1.0 squeeze.26
  171.1 0.6 bitcast_dynamic-update-slice_fusion.7
  171.7 3.8 %collective-permute-start.3 = (bf16[1,128,384]{2,1,0:T(8,128)(2,1)}, bf16[1,128,384]{2,1,0:T(8,128)(2,1)S(1)}, u32[]{:S(2)}, u32[]{:S(2)}) collective-permute-start(bf16[1,128,384]{2,1,0:T(8,128)(2,1)} %collective-permute-done.1), channel_id=1, source_target_pairs={{0,448},{64,0},{128,64},{192,128},{256,192},{320,256},{384,320},{4... | collective-permute-start | bytes 294920 | tf_op jit(solution)/shard_map/ppermute | solution.py:16
  175.5 0.0 collective-permute-done
  175.5 1.9 collective-permute-start.2
  177.4 1.5 bitcast_dynamic-update-slice_fusion.6
  179.0 1.5 bitcast_dynamic-update-slice_fusion.5
  180.5 4.6 %collective-permute-start.5 = (bf16[1,128,384]{2,1,0:T(8,128)(2,1)S(1)}, bf16[1,128,384]{2,1,0:T(8,128)(2,1)S(1)}, u32[]{:S(2)}, u32[]{:S(2)}) collective-permute-start(bf16[1,128,384]{2,1,0:T(8,128)(2,1)S(1)} %collective-permute-done.3), channel_id=1, source_target_pairs={{0,448},{64,0},{128,64},{192,128},{256,192},{320,256},{384,320},{4... | collective-permute-start | bytes 294920 | tf_op jit(solution)/shard_map/ppermute | solution.py:16
  185.1 0.0 collective-permute-done.2
  185.1 1.9 collective-permute-start.4
  187.0 0.6 bitcast_dynamic-update-slice_fusion.4
  187.7 0.7 bitcast_dynamic-update-slice_fusion.3
  188.3 3.3 collective-permute-done.4
  191.7 2.1 collective-permute-start.6
  193.8 0.7 bitcast_dynamic-update-slice_fusion.2
  194.4 0.7 bitcast_dynamic-update-slice_fusion.1
  195.1 3.1 collective-permute-done.6
  198.2 0.7 bitcast_dynamic-update-slice_fusion
  198.9 2.2 reshape.101
  201.1 6.1 %fusion.10 = f32[1152,768]{0,1:T(8,128)} fusion(bf16[1152,1024]{1,0:T(8,128)(2,1)} %reshape.101, bf16[1024,384]{1,0:T(8,128)(2,1)} %bitcast.48, bf16[1024,384]{1,0:T(8,128)(2,1)} %bitcast_dynamic-update-slice_fusion), kind=kOutput, calls=%fused_computation.24 | convolution fusion | flops 1815085056 | bytes 7471104 | tf_op jit(solution)/shard_map/dot_general | solution.py:34
  207.2 2.9 reshape.98
  210.2 1.4 copy-done.2
  211.6 3.4 convolution_convert_fusion.2
  215.0 3.4 multiply_convert_fusion.2
  218.4 3.3 convolution_convert_fusion.1
  221.8 3.2 convolution_convert_fusion
  225.0 2.4 reshape.102
  227.4 22.3 %all-to-all-start.2 = ((bf16[64,18,1024]{2,1,0:T(8,128)(2,1)}), bf16[64,18,1024]{2,1,0:T(8,128)(2,1)}, u32[]{:S(2)}, u32[]{:S(2)}) async-start(bf16[64,18,1024]{2,1,0:T(8,128)(2,1)} %reshape.102), calls=%async_computation.2 | async-start | bytes 6291456 | tf_op jit(solution)/shard_map/all_to_all | solution.py:89
  249.7 0.3 reduce-scatter.4.cloned.1.call-start
  250.0 1.6 pad_maximum_fusion
  251.6 2.6 copy.31
  254.2 0.0 reduce-scatter.4.cloned.1.call-update
  254.2 68.9 %all-to-all-done.2 = bf16[64,18,1024]{2,1,0:T(8,128)(2,1)} async-done(((bf16[64,18,1024]{2,1,0:T(8,128)(2,1)}), bf16[64,18,1024]{2,1,0:T(8,128)(2,1)}, u32[]{:S(2)}, u32[]{:S(2)}) %all-to-all-start.2) | async-done | bytes 2359328 | tf_op jit(solution)/shard_map/all_to_all | solution.py:89
  323.2 2.9 reshape.103
  326.1 5.4 %gather_fusion = bf16[1024,1024]{1,0:T(8,128)(2,1)} fusion(bf16[1152,1024]{1,0:T(8,128)(2,1)S(1)} %reshape.103, s32[1024]{0:T(1024)S(1)} %broadcast_clamp_fusion), kind=kCustom, calls=%fused_computation | custom fusion | bytes 4198400 | tf_op jit(solution)/shard_map/gather | solution.py:96
  331.5 3.7 %bitcast_reduce_fusion = bf16[128,1024]{1,0:T(8,128)(2,1)} fusion(bf16[1024,1024]{1,0:T(8,128)(2,1)} %gather_fusion), kind=kLoop, calls=%fused_computation.8 | loop fusion | flops 917504 | bytes 2359296 | tf_op jit(solution)/shard_map/reduce_sum | solution.py:99
  335.2 1.2 copy.32
  336.4 0.7 slice_bitcast_fusion
  337.1 0.8 copy.30
  337.9 0.8 copy.29
  (24 shorter events, 0.1 us)
Async XLA Ops:
  7.2 2.8 copy-start
  18.4 11.8 %copy-start.7 = (f32[128,8]{0,1:T(8,128)S(1)}, f32[128,8]{0,1:T(8,128)}, u32[]{:S(2)}) copy-start(f32[128,8]{0,1:T(8,128)} %param.9) | copy-start | bytes 12292
  18.4 85.3 %all-to-all-start.1 = ((bf16[64,18,1024]{2,1,0:T(8,128)(2,1)}), bf16[64,18,1024]{2,1,0:T(8,128)(2,1)S(1)}, u32[]{:S(2)}, u32[]{:S(2)}) async-start(bf16[64,18,1024]{2,1,0:T(8,128)(2,1)} %reshape.100), calls=%async_computation.1 | async-start | bytes 6291456 | tf_op jit(solution)/shard_map/all_to_all | solution.py:83
  44.2 78.4 %copy-start.5 = (bf16[1,128,384]{2,1,0:T(8,128)(2,1)S(1)}, bf16[1,128,384]{2,1,0:T(8,128)(2,1)}, u32[]{:S(2)}) copy-start(bf16[1,128,384]{2,1,0:T(8,128)(2,1)} %param.12) | copy-start | bytes 294916
  103.6 103.6 %all-to-all-start = ((bf16[64,18,1024]{2,1,0:T(8,128)(2,1)}), bf16[64,18,1024]{2,1,0:T(8,128)(2,1)}, u32[]{:S(2)}, u32[]{:S(2)}) async-start(bf16[64,18,1024]{2,1,0:T(8,128)(2,1)} %reshape.97), calls=%async_computation | async-start | bytes 6291456 | tf_op jit(solution)/shard_map/all_to_all | solution.py:84
  109.9 61.8 %collective-permute-start.1 = (bf16[1,128,384]{2,1,0:T(8,128)(2,1)}, bf16[1,128,384]{2,1,0:T(8,128)(2,1)}, u32[]{:S(2)}, u32[]{:S(2)}) collective-permute-start(bf16[1,128,384]{2,1,0:T(8,128)(2,1)} %param.11), channel_id=1, source_target_pairs={{0,448},{64,0},{128,64},{192,128},{256,192},{320,256},{384,320},{4... | collective-permute-start | bytes 294920 | tf_op jit(solution)/shard_map/ppermute | solution.py:16
  120.6 54.9 %collective-permute-start = (bf16[1,128,384]{2,1,0:T(8,128)(2,1)}, bf16[1,128,384]{2,1,0:T(8,128)(2,1)}, u32[]{:S(2)}, u32[]{:S(2)}) collective-permute-start(bf16[1,128,384]{2,1,0:T(8,128)(2,1)} %param.11), channel_id=1, source_target_pairs={{0,64},{64,128},{128,192},{192,256},{256,320},{320,384},{384,448},... | collective-permute-start | bytes 294920 | tf_op jit(solution)/shard_map/ppermute | solution.py:13
  122.5 48.5 %copy-start.6 = (bf16[1,128,384]{2,1,0:T(8,128)(2,1)S(1)}, bf16[1,128,384]{2,1,0:T(8,128)(2,1)}, u32[]{:S(2)}) copy-start(bf16[1,128,384]{2,1,0:T(8,128)(2,1)} %param.11) | copy-start | bytes 294916
  171.7 8.8 %collective-permute-start.3 = (bf16[1,128,384]{2,1,0:T(8,128)(2,1)}, bf16[1,128,384]{2,1,0:T(8,128)(2,1)S(1)}, u32[]{:S(2)}, u32[]{:S(2)}) collective-permute-start(bf16[1,128,384]{2,1,0:T(8,128)(2,1)} %collective-permute-done.1), channel_id=1, source_target_pairs={{0,448},{64,0},{128,64},{192,128},{256,192},{320,256},{384,320},{4... | collective-permute-start | bytes 294920 | tf_op jit(solution)/shard_map/ppermute | solution.py:16
  175.5 9.6 %collective-permute-start.2 = (bf16[1,128,384]{2,1,0:T(8,128)(2,1)}, bf16[1,128,384]{2,1,0:T(8,128)(2,1)S(1)}, u32[]{:S(2)}, u32[]{:S(2)}) collective-permute-start(bf16[1,128,384]{2,1,0:T(8,128)(2,1)} %collective-permute-done), channel_id=1, source_target_pairs={{0,64},{64,128},{128,192},{192,256},{256,320},{320,384},{384,448},... | collective-permute-start | bytes 294920 | tf_op jit(solution)/shard_map/ppermute | solution.py:13
  180.5 13.9 %collective-permute-start.5 = (bf16[1,128,384]{2,1,0:T(8,128)(2,1)S(1)}, bf16[1,128,384]{2,1,0:T(8,128)(2,1)S(1)}, u32[]{:S(2)}, u32[]{:S(2)}) collective-permute-start(bf16[1,128,384]{2,1,0:T(8,128)(2,1)S(1)} %collective-permute-done.3), channel_id=1, source_target_pairs={{0,448},{64,0},{128,64},{192,128},{256,192},{320,256},{384,320},{4... | collective-permute-start | bytes 294920 | tf_op jit(solution)/shard_map/ppermute | solution.py:16
  185.1 6.6 %collective-permute-start.4 = (bf16[1,128,384]{2,1,0:T(8,128)(2,1)S(1)}, bf16[1,128,384]{2,1,0:T(8,128)(2,1)S(1)}, u32[]{:S(2)}, u32[]{:S(2)}) collective-permute-start(bf16[1,128,384]{2,1,0:T(8,128)(2,1)S(1)} %collective-permute-done.2), channel_id=1, source_target_pairs={{0,64},{64,128},{128,192},{192,256},{256,320},{320,384},{384,448},... | collective-permute-start | bytes 294920 | tf_op jit(solution)/shard_map/ppermute | solution.py:13
  191.7 6.6 %collective-permute-start.6 = (bf16[1,128,384]{2,1,0:T(8,128)(2,1)S(1)}, bf16[1,128,384]{2,1,0:T(8,128)(2,1)S(1)}, u32[]{:S(2)}, u32[]{:S(2)}) collective-permute-start(bf16[1,128,384]{2,1,0:T(8,128)(2,1)S(1)} %collective-permute-done.4), channel_id=1, source_target_pairs={{0,64},{64,128},{128,192},{192,256},{256,320},{320,384},{384,448},... | collective-permute-start | bytes 294920 | tf_op jit(solution)/shard_map/ppermute | solution.py:13
  210.1 1.4 copy-start.2
  211.6 3.4 copy-start.4
  211.6 3.4 copy-start.8
  215.0 3.4 copy-start.1
  218.4 3.3 copy-start.3
  227.4 95.8 %all-to-all-start.2 = ((bf16[64,18,1024]{2,1,0:T(8,128)(2,1)}), bf16[64,18,1024]{2,1,0:T(8,128)(2,1)}, u32[]{:S(2)}, u32[]{:S(2)}) async-start(bf16[64,18,1024]{2,1,0:T(8,128)(2,1)} %reshape.102), calls=%async_computation.2 | async-start | bytes 6291456 | tf_op jit(solution)/shard_map/all_to_all | solution.py:89
  249.7 85.5 %reduce-scatter.4.cloned.1.call-start = ((), (), s32[]{:S(2)}) async-start(), calls=%async_computation.4 | async-start | bytes 2654208
Sparse Core Ops, SparseCore 0:
  254.3 39.2 reduce-scatter.3
